TPU v7x, 32 devices: a whole 2x2x4 slice. The times are simulated.
32 devices in a mesh: parts: 2 (over y), space: 4 (over z), mem: 4 (over x, core).
Axes of the slice: x: 2, y: 2, z: 4, core: 2. Of those that a mesh axis runs over, the one named last changes fastest.
Arguments:
- prior_replicas: float32 [128, 2, 32, 2048], P(('parts', 'mem'), None, 'space'), parts along dimension 0, may hold values from -6 to 6
- wind_field: float32 [4, 2, 32, 2048], P('parts', None, 'space'), parts along dimension 0, may hold values from -0.4 to 0.4
- obs_index: int32 [16384], P(('parts', 'space')), parts along dimension 0, may hold values from 0 to 32767, as said below
- obs_count: int32 [8], P(('parts', 'space')), parts along dimension 0, may hold values from 256 to 2048, as said below
- obs_value: float32 [16384], P(('parts', 'space')), parts along dimension 0, may hold values from -6 to 6
- obs_weight: float32 [16384], P(('parts', 'space')), parts along dimension 0, may hold values from 0.05 to 0.5
Outputs:
- analysis: float32 [128, 2, 32, 2048], P(('parts', 'mem'), None, 'space'), parts along dimension 0
There are 2 independent parts, one for each index of `parts`. A program takes and returns all parts, laid end to end along the dimension named above; each array names one. Nothing has to cross between parts.
Inputs may be any that keep to these rules, and one draw needn't show every extreme that they name: `obs_index`: the slots of one strip name distinct cells of that strip, as f * 8 * 2048 + r * 2048 + c for field f, local row r and column c. `obs_count`: one entry per strip; some strip uses all 2048 slots.
All inputs are finite; a program needn't handle non-finite values.
Results may differ from a plain program's by a relative error of at most 0.0038.
Values may be sent and summed in bfloat16 or wider, within the bound.
No kernel may reach another device: no remote copies, remote signals or barrier semaphores. Data moves between devices by JAX's collectives and lax.ppermute only.
A program may use at most 128 MiB of HBM per device.

v0:
```python
import jax
import jax.numpy as jnp
from jax import lax
from jax.sharding import PartitionSpec as P

REPLICA_COUNT = 64
NS_ITERS = 5
DIFFUSION = (0.05, 0.15)


def padded(value, sides, width):
    for axis, dim in sides:
        peers, length = (lax.axis_size(axis), value.shape[dim])
        up = [(i, (i + 1) % peers) for i in range(peers - 1)]
        down = [(j, i) for i, j in up]
        last = lax.slice_in_dim(value, length - width, length, axis=dim)
        initial = lax.slice_in_dim(value, 0, width, axis=dim)
        before = lax.ppermute(last, axis, up)
        after = lax.ppermute(initial, axis, down)
        value = jnp.concatenate([before, value, after], axis=dim)
    return value


def shift_columns(field, offset):
    width = field.shape[-1]
    blank = jnp.zeros(field.shape[:-1] + (abs(offset),), field.dtype)
    if offset > 0:
        return jnp.concatenate([field[..., offset:], blank], -1)
    return jnp.concatenate([blank, field[..., : width + offset]], -1)


def advance(extended, wind_rows):
    center = extended[:, :, 2:-2]
    north_one = extended[:, :, 3:-1]
    south_one = extended[:, :, 1:-3]
    north_two = extended[:, :, 4:]
    south_two = extended[:, :, :-4]
    east_one = shift_columns(center, 1)
    west_one = shift_columns(center, -1)
    east_two = shift_columns(center, 2)
    west_two = shift_columns(center, -2)
    grad_row = (8.0 * (north_one - south_one) - (north_two - south_two)) / 12.0
    grad_col = (8.0 * (east_one - west_one) - (east_two - west_two)) / 12.0
    laplace = north_one + south_one + east_one + west_one - 4.0 * center
    diffusion = jnp.array(DIFFUSION, jnp.float32).reshape(2, 1, 1)
    return center - wind_rows[0] * grad_row - wind_rows[1] * grad_col + diffusion * laplace


def shard_terms(observed, slot_weight, obs_value):
    obs_mean = jnp.sum(observed, 0) / REPLICA_COUNT
    obs_anomaly = observed - obs_mean
    weighted = obs_anomaly * slot_weight
    gram = jnp.dot(
        weighted, obs_anomaly.T, precision=lax.Precision.HIGHEST, preferred_element_type=jnp.float32
    )
    drive = jnp.dot(
        weighted,
        obs_value - obs_mean,
        precision=lax.Precision.HIGHEST,
        preferred_element_type=jnp.float32,
    )
    return (gram, drive)


def ensemble_weights(gram, drive):
    ident = jnp.eye(REPLICA_COUNT, dtype=jnp.float32)
    system = (REPLICA_COUNT - 1.0) * ident + gram
    scale = jnp.sqrt(jnp.sum(system * system))

    def newton_turn(turn, carry):
        root, inverse_root = carry
        middle_term = 0.5 * (
            3.0 * ident
            - jnp.dot(
                inverse_root,
                root,
                precision=lax.Precision.HIGHEST,
                preferred_element_type=jnp.float32,
            )
        )
        root = jnp.dot(
            root, middle_term, precision=lax.Precision.HIGHEST, preferred_element_type=jnp.float32
        )
        inverse_root = jnp.dot(
            middle_term,
            inverse_root,
            precision=lax.Precision.HIGHEST,
            preferred_element_type=jnp.float32,
        )
        return (root, inverse_root)

    root, inverse_root = lax.fori_loop(0, NS_ITERS, newton_turn, (system / scale, ident))
    half = inverse_root / jnp.sqrt(scale)
    precision_matrix = jnp.dot(
        half, half, precision=lax.Precision.HIGHEST, preferred_element_type=jnp.float32
    )
    mean_weight = jnp.dot(
        precision_matrix, drive, precision=lax.Precision.HIGHEST, preferred_element_type=jnp.float32
    )
    spread = jnp.sqrt(REPLICA_COUNT - 1.0) * half
    return (mean_weight[:, None] + spread).astype(jnp.bfloat16)


def local(prior_replicas, wind_field, obs_index, obs_count, obs_value, obs_weight):
    member_count, field_count, row_count, col_count = prior_replicas.shape
    state = prior_replicas
    for step_index in range(2):
        extended = padded(state, (("space", 2),), 2)
        state = advance(extended, wind_field[step_index])
    capacity = obs_index.shape[0]
    raveled_vector = state.reshape(member_count, -1)
    local_obs = jnp.take(raveled_vector, obs_index, axis=1)
    slot_number = jnp.arange(capacity, dtype=jnp.int32)
    slot_weight = obs_weight * (slot_number < obs_count[0]).astype(jnp.float32)
    gathered = lax.all_gather(local_obs, "mem", axis=0, tiled=True)
    gram, drive = shard_terms(gathered, slot_weight, obs_value)
    gram, drive = lax.psum((gram, drive), "space")
    transform = ensemble_weights(gram, drive)
    transform_rows = transform.T
    block = lax.all_to_all(state, "mem", split_axis=3, concat_axis=0, tiled=True)
    replica_centroid = jnp.sum(block, 0) / REPLICA_COUNT
    replica_departure = (block - replica_centroid).astype(jnp.bfloat16)
    posterior_correction = jnp.dot(
        transform_rows,
        replica_departure.reshape(REPLICA_COUNT, -1),
        preferred_element_type=jnp.float32,
    )
    analysed = posterior_correction.reshape(block.shape) + replica_centroid
    return lax.all_to_all(analysed, "mem", split_axis=0, concat_axis=3, tiled=True)


def solution(mesh):
    in_specs = (
        P(("parts", "mem"), None, "space", None),
        P("parts", None, "space", None),
        P(("parts", "space")),
        P(("parts", "space")),
        P(("parts", "space")),
        P(("parts", "space")),
    )
    out_specs = P(("parts", "mem"), None, "space", None)
    return jax.shard_map(local, mesh=mesh, in_specs=in_specs, out_specs=out_specs, check_vma=False)
```

profile of v0, /device:TPU:0, one launch (start us, length us, event | category | flops | bytes accessed | tf_op | source)
XLA Modules:
  0.0 220.6 jit_solution(2224251359348248009)
XLA Ops:
  0.0 2.8 %fusion.44 = (f32[16,2,2,2048]{3,2,1,0:T(2,128)S(1)}, f32[16,2,2,2048]{3,2,1,0:T(2,128)S(1)}) fusion(f32[16,2,8,2048]{3,2,1,0:T(8,128)} %param.10), kind=kLoop, calls=%fused_computation.77 | loop fusion | bytes 2097152 | tf_op jit(solution)/shard_map/slice | solution.py:17
  2.9 1.1 copy.66
  4.0 5.7 %collective-permute-start.1 = (f32[16,2,2,2048]{3,0,2,1:T(8,128)}, f32[16,2,2,2048]{3,0,2,1:T(8,128)}, u32[]{:S(2)}, u32[]{:S(2)}) collective-permute-start(f32[16,2,2,2048]{3,0,2,1:T(8,128)} %copy.66), channel_id=1, source_target_pairs={{0,4},{4,8},{8,12},{1,5},{5,9},{9,13},{2,6},{6,10},{10,14},{3,7},{... | collective-permute-start | bytes 1572872 | tf_op jit(solution)/shard_map/ppermute | solution.py:18
  9.7 0.3 copy.67
  10.0 1.3 collective-permute-start
  11.3 0.8 fusion.43
  12.1 0.8 fusion.42
  12.9 2.5 %copy.68 = f32[16,2,8,2046]{3,0,2,1:T(8,128)} copy(f32[16,2,8,2046]{3,2,1,0:T(8,128)S(1)} %get-tuple-element.65) | data formatting | bytes 4190208
  15.4 2.6 %copy.69 = f32[16,2,8,2046]{3,0,2,1:T(8,128)} copy(f32[16,2,8,2046]{3,2,1,0:T(8,128)S(1)} %get-tuple-element.64) | data formatting | bytes 4190208
  18.0 2.5 %copy.70 = f32[16,2,8,2047]{3,0,2,1:T(8,128)} copy(f32[16,2,8,2047]{3,2,1,0:T(8,128)S(1)} %get-tuple-element.63) | data formatting | bytes 4192256
  20.5 2.6 %copy.71 = f32[16,2,8,2047]{3,0,2,1:T(8,128)} copy(f32[16,2,8,2047]{3,2,1,0:T(8,128)S(1)} %get-tuple-element.62) | data formatting | bytes 4192256
  23.8 1.2 constant_dynamic-update-slice_fusion.3
  25.1 1.2 constant_dynamic-update-slice_fusion.1
  26.4 0.4 copy-done.1
  26.8 0.6 copy-done.2
  27.4 0.6 copy-done.3
  28.0 4.0 %fusion.15 = f32[16,2,8,2048]{3,0,2,1:T(8,128)S(1)} fusion(f32[16,2,10,2048]{3,0,2,1:T(8,128)S(1)} %get-tuple-element.69, f32[16,2,10,2048]{3,0,2,1:T(8,128)S(1)} %constant_dynamic-update-slice_fusion, f32[16,2,8,2046]{3,0,2,1:T(8,128)S(1)} %copy-done.1, f32[16,2,8,2046]{3,0,2,1:T(8,128)S(1)} %copy-done.2, f32[16,2,8,2047]{3,0,2,1:T(8,128)S(1)} %copy-done.3, ...), kind=kLoop, calls=%fused_computation.25 | loop fusion | flops 9961472 | bytes 21096456 | tf_op jit(solution)/shard_map/add | solution.py:46
  32.0 0.8 fusion.39
  32.9 1.3 collective-permute-start.2
  34.2 5.4 %collective-permute-start.3 = (f32[16,2,2,2048]{3,0,2,1:T(8,128)S(1)}, f32[16,2,2,2048]{3,0,2,1:T(8,128)S(1)}, u32[]{:S(2)}, u32[]{:S(2)}) collective-permute-start(f32[16,2,2,2048]{3,0,2,1:T(8,128)S(1)} %get-tuple-element.61), channel_id=1, source_target_pairs={{0,4},{4,8},{8,12},{1,5},{5,9},{9,13},{2,6},{6,10},{10,14},{3,7},{... | collective-permute-start | bytes 1572872 | tf_op jit(solution)/shard_map/ppermute | solution.py:18
  39.6 0.8 fusion.40
  40.3 8.4 %collective-permute-done.2 = f32[16,2,2,2048]{3,0,2,1:T(8,128)S(1)} collective-permute-done((f32[16,2,2,2048]{3,0,2,1:T(8,128)S(1)}, f32[16,2,2,2048]{3,0,2,1:T(8,128)S(1)}, u32[]{:S(2)}, u32[]{:S(2)}) %collective-permute-start.2) | collective-permute-done | bytes 524320 | tf_op jit(solution)/shard_map/ppermute | solution.py:19
  48.8 1.2 collective-permute-done.3
  49.9 2.5 %fusion.10 = f32[16,2,8,2048]{3,0,2,1:T(8,128)S(1)} fusion(f32[16,2,8,2048]{3,0,2,1:T(8,128)S(1)} %fusion.15, f32[16,2,2,2048]{3,0,2,1:T(8,128)S(1)} %collective-permute-done.3, f32[16,2,2,2048]{3,0,2,1:T(8,128)S(1)} %collective-permute-done.2, f32[16,2,8,2046]{3,0,2,1:T(8,128)S(1)} %get-tuple-element.59, f32[16,2,8,2046]{3,0,2,1:T(8,128)S(1)} %get-tuple-element.58, ...), kind=kLoop, calls=%fused_computation.18 | loop fusion | flops 12058624 | bytes 13756424 | tf_op jit(solution)/shard_map/add | solution.py:46
  52.5 8.5 %copy.48 = f32[16,2,8,2048]{0,3,2,1:T(8,128)} copy(f32[16,2,8,2048]{3,0,2,1:T(8,128)S(1)} %fusion.10) | data formatting | bytes 4194304 | tf_op jit(solution)/shard_map/add | solution.py:46
  61.0 11.1 %copy.51 = f32[16,2,8,2048]{0,2,1,3:T(8,128)} copy(f32[16,2,8,2048]{3,0,2,1:T(8,128)S(1)} %fusion.10) | data formatting | bytes 4194304 | tf_op jit(solution)/shard_map/add | solution.py:46
  72.1 11.2 %gather_fusion = f32[2048,16]{1,0:T(8,128)S(1)} fusion(f32[16,32768]{0,1:T(8,128)} %bitcast.70, s32[2048]{0:T(1024)S(1)} %fusion.34), kind=kCustom, calls=%fused_computation | custom fusion | bytes 270336 | tf_op jit(solution)/shard_map/jit(_take)/gather | solution.py:112
  83.3 0.3 select_bitcast_fusion
  83.7 0.3 copy.49
  84.0 7.2 %all_gather.3 = f32[64,2048]{1,0:T(8,128)S(1)} all-gather(f32[16,2048]{1,0:T(8,128)S(1)} %copy.49), channel_id=1, replica_groups=mesh['parts'=2,'space'=4,'mem'=4] {'mem'}, dimensions={0}, use_global_device_ids=true | all-gather | bytes 655360 | tf_op jit(solution)/shard_map/all_gather | solution.py:115
  91.2 0.6 fusion.18
  91.8 0.5 convolution_bitcast_fusion.2
  92.3 19.9 %all-reduce.8 = (f32[64,64]{1,0:T(8,128)S(1)}, f32[64]{0:T(128)S(1)}) all-reduce(f32[64,64]{1,0:T(8,128)S(1)} %fusion.18, f32[64]{0:T(128)S(1)} %convolution_bitcast_fusion.2), channel_id=1, replica_groups=mesh['parts'=2,'space'=4,'mem'=4] {'space'}, use_global_device_ids=true, to_apply=%region_1.2 | all-reduce | flops 4160 | bytes 33280 | tf_op jit(solution)/shard_map/psum | solution.py:117
  112.3 0.6 multiply_reduce_fusion
  113.7 10.1 %reshape.58 = f32[4,1,131072]{2,1,0:T(1,128)} reshape(f32[2048,2,8,16]{3,2,1,0:T(8,128)} %bitcast.68) | data formatting | bytes 4194304
  123.8 3.8 %all-to-all-start = ((f32[4,1,131072]{2,1,0:T(1,128)}), f32[4,1,131072]{2,1,0:T(1,128)S(1)}, u32[]{:S(2)}, u32[]{:S(2)}) async-start(f32[4,1,131072]{2,1,0:T(1,128)} %reshape.58), calls=%async_computation | async-start | bytes 4194304 | tf_op jit(solution)/shard_map/all_to_all | solution.py:120
  127.6 3.2 %while.13 = (s32[]{:T(128)}, f32[64,64]{0,1:T(8,128)S(1)}, f32[64,64]{1,0:T(8,128)S(1)}, s32[]{:T(128)}) while((s32[]{:T(128)}, f32[64,64]{0,1:T(8,128)S(1)}, f32[64,64]{1,0:T(8,128)S(1)}, s32[]{:T(128)}) %tuple.37), condition=%wide.region_4.5_spmd.clone, body=%wide.region_3.4_spmd.clone.sunk | while | flops 9453570 | bytes 213045 | solution.py:92
  127.7 0.2 fusion.68
  127.9 0.2 fusion.69
  128.0 0.2 convolution_bitcast_fusion.4
  128.3 0.2 fusion.68
  128.7 0.2 convolution_bitcast_fusion.4
  128.9 0.2 fusion.68
  129.1 0.2 fusion.69
  129.3 0.2 convolution_bitcast_fusion.4
  129.6 0.2 fusion.68
  130.0 0.2 convolution_bitcast_fusion.4
  130.2 0.2 fusion.68
  130.4 0.2 fusion.69
  130.6 0.2 convolution_bitcast_fusion.4
  130.9 0.2 fusion.32
  131.2 21.9 %all-to-all-done = f32[4,1,131072]{2,1,0:T(1,128)S(1)} async-done(((f32[4,1,131072]{2,1,0:T(1,128)}), f32[4,1,131072]{2,1,0:T(1,128)S(1)}, u32[]{:S(2)}, u32[]{:S(2)}) %all-to-all-start) | async-done | bytes 2097184 | tf_op jit(solution)/shard_map/all_to_all | solution.py:120
  153.1 1.3 copy-done.5
  154.4 0.5 broadcast.101
  154.9 7.7 %reduce.1 = f32[4,131072]{1,0:T(4,128)S(1)} reduce(f32[4,1,131072]{2,1,0:T(1,128)} %copy-done.5, f32[]{:T(128)} %broadcast.101), dimensions={1}, to_apply=%all_to_all.26.reduce_sub_computation | reduce | bytes 4194308 | tf_op jit(solution)/shard_map/all_to_all | solution.py:120
  162.6 11.5 %reshape.59 = f32[2048,2,8,16]{3,2,1,0:T(8,128)} reshape(f32[4,131072]{1,0:T(4,128)S(1)} %reduce.1) | data formatting | bytes 4194304
  174.2 10.2 %copy.52 = f32[16,2,8,4,512]{4,2,1,0,3:T(8,128)S(1)} copy(f32[16,2,8,4,512]{0,2,1,4,3:T(8,128)} %bitcast.69) | data formatting | bytes 4194304 | tf_op jit(solution)/shard_map/all_to_all | solution.py:120
  184.6 1.5 all_to_all.29
  186.1 1.7 subtract_convert_fusion
  187.9 0.4 copy.60
  188.2 1.5 convolution_add_fusion
  189.7 1.2 copy.55
  190.9 28.2 %all_to_all.36 = f32[64,2,8,512]{3,2,1,0:T(8,128)S(1)} all-to-all(f32[64,2,8,512]{3,2,1,0:T(8,128)S(1)} %copy.55), channel_id=1, replica_groups=mesh['parts'=2,'space'=4,'mem'=4] {'mem'}, dimensions={0} | all-to-all | bytes 4194304 | tf_op jit(solution)/shard_map/all_to_all | solution.py:129
  219.1 1.5 copy.56
  (47 shorter events, 1.0 us)
Async XLA Ops:
  0.0 11.3 %copy-start = (f32[16,2,8,2048]{3,2,1,0:T(8,128)S(1)}, f32[16,2,8,2048]{3,2,1,0:T(8,128)}, u32[]{:S(2)}) copy-start(f32[16,2,8,2048]{3,2,1,0:T(8,128)} %param.10) | copy-start | bytes 6291460
  4.0 19.8 %collective-permute-start.1 = (f32[16,2,2,2048]{3,0,2,1:T(8,128)}, f32[16,2,2,2048]{3,0,2,1:T(8,128)}, u32[]{:S(2)}, u32[]{:S(2)}) collective-permute-start(f32[16,2,2,2048]{3,0,2,1:T(8,128)} %copy.66), channel_id=1, source_target_pairs={{0,4},{4,8},{8,12},{1,5},{5,9},{9,13},{2,6},{6,10},{10,14},{3,7},{... | collective-permute-start | bytes 1572872 | tf_op jit(solution)/shard_map/ppermute | solution.py:18
  10.0 16.3 %collective-permute-start = (f32[16,2,2,2048]{3,0,2,1:T(8,128)S(1)}, f32[16,2,2,2048]{3,0,2,1:T(8,128)S(1)}, u32[]{:S(2)}, u32[]{:S(2)}) collective-permute-start(f32[16,2,2,2048]{3,0,2,1:T(8,128)S(1)} %copy.67), channel_id=1, source_target_pairs={{4,0},{8,4},{12,8},{5,1},{9,5},{13,9},{6,2},{10,6},{14,10},{7,3},{... | collective-permute-start | bytes 1572872 | tf_op jit(solution)/shard_map/ppermute | solution.py:19
  12.1 0.8 copy-start.7
  20.5 3.2 %copy-start.8 = (f32[2048]{0:T(1024)S(1)}, f32[2048]{0:T(1024)}, u32[]{:S(2)}) copy-start(f32[2048]{0:T(1024)} %param.15) | copy-start | bytes 24580
  20.5 3.2 %copy-start.6 = (f32[2,2,8,2048]{3,2,1,0:T(8,128)S(1)}, f32[2,2,8,2048]{3,2,1,0:T(8,128)}, u32[]{:S(2)}) copy-start(f32[2,2,8,2048]{3,2,1,0:T(8,128)} %param.11) | copy-start | bytes 786436
  23.8 2.6 %copy-start.4 = (f32[16,2,8,2047]{3,0,2,1:T(8,128)S(1)}, f32[16,2,8,2047]{3,0,2,1:T(8,128)}, u32[]{:S(2)}) copy-start(f32[16,2,8,2047]{3,0,2,1:T(8,128)} %copy.71) | copy-start | bytes 6288388
  25.1 1.7 copy-start.1
  25.1 2.3 %copy-start.2 = (f32[16,2,8,2046]{3,0,2,1:T(8,128)S(1)}, f32[16,2,8,2046]{3,0,2,1:T(8,128)}, u32[]{:S(2)}) copy-start(f32[16,2,8,2046]{3,0,2,1:T(8,128)} %copy.69) | copy-start | bytes 6285316
  25.1 2.9 %copy-start.3 = (f32[16,2,8,2047]{3,0,2,1:T(8,128)S(1)}, f32[16,2,8,2047]{3,0,2,1:T(8,128)}, u32[]{:S(2)}) copy-start(f32[16,2,8,2047]{3,0,2,1:T(8,128)} %copy.70) | copy-start | bytes 6288388
  25.1 2.9 %copy-start.10 = (f32[2]{0:T(128)S(1)}, f32[2]{0:T(128)}, u32[]{:S(2)}) copy-start(f32[2]{0:T(128)} %constant.52.clone) | copy-start | bytes 28
  32.9 15.9 %collective-permute-start.2 = (f32[16,2,2,2048]{3,0,2,1:T(8,128)S(1)}, f32[16,2,2,2048]{3,0,2,1:T(8,128)S(1)}, u32[]{:S(2)}, u32[]{:S(2)}) collective-permute-start(f32[16,2,2,2048]{3,0,2,1:T(8,128)S(1)} %get-tuple-element.60), channel_id=1, source_target_pairs={{4,0},{8,4},{12,8},{5,1},{9,5},{13,9},{6,2},{10,6},{14,10},{7,3},{... | collective-permute-start | bytes 1572872 | tf_op jit(solution)/shard_map/ppermute | solution.py:19
  34.2 15.8 %collective-permute-start.3 = (f32[16,2,2,2048]{3,0,2,1:T(8,128)S(1)}, f32[16,2,2,2048]{3,0,2,1:T(8,128)S(1)}, u32[]{:S(2)}, u32[]{:S(2)}) collective-permute-start(f32[16,2,2,2048]{3,0,2,1:T(8,128)S(1)} %get-tuple-element.61), channel_id=1, source_target_pairs={{0,4},{4,8},{8,12},{1,5},{5,9},{9,13},{2,6},{6,10},{10,14},{3,7},{... | collective-permute-start | bytes 1572872 | tf_op jit(solution)/shard_map/ppermute | solution.py:18
  83.3 7.9 %copy-start.9 = (f32[2048]{0:T(1024)S(1)}, f32[2048]{0:T(1024)}, u32[]{:S(2)}) copy-start(f32[2048]{0:T(1024)} %param.14) | copy-start | bytes 24580
  123.8 29.3 %all-to-all-start = ((f32[4,1,131072]{2,1,0:T(1,128)}), f32[4,1,131072]{2,1,0:T(1,128)S(1)}, u32[]{:S(2)}, u32[]{:S(2)}) async-start(f32[4,1,131072]{2,1,0:T(1,128)} %reshape.58), calls=%async_computation | async-start | bytes 4194304 | tf_op jit(solution)/shard_map/all_to_all | solution.py:120
  153.1 1.3 copy-start.5
where the time goes:
time: 221 us
  local copies, waits for them, and re-layouts  91.4 us (41%)
  blocking collectives  55.3 us (25%)
  waiting for transfers between devices  31.5 us (14%)
  starting transfers between devices  17.5 us (8%)
  other arithmetic  17.1 us (8%)
  matrix products  5.81 us (3%)
    unnamed x35, local copies, waits for them, and re-layouts  39.1 us
    all_to_all x1, blocking collectives, local(): lax.all_to_all(analysed, 'mem', split_axis=0, concat_axis=3, tiled=True)  28.2 us
    all_to_all x1, waiting for transfers between devices, local(): lax.all_to_all(state, 'mem', split_axis=3, concat_axis=0, tiled=True)  21.9 us
    psum x1, blocking collectives, local(): gram, drive = lax.psum((gram, drive), 'space')  19.9 us
    add x2, local copies, waits for them, and re-layouts, advance(): center - wind_rows[0] * grad_row - wind_rows[1] * grad_col  19.6 us
    all_to_all x3, local copies, waits for them, and re-layouts, local(): lax.all_to_all(state, 'mem', split_axis=3, concat_axis=0, tiled=True)  12.3 us
    gather x1, local copies, waits for them, and re-layouts, local(): local_obs = jnp.take(raveled_vector, obs_index, axis=1)  11.2 us
    ppermute x2, starting transfers between devices, padded(): before = lax.ppermute(last, axis, up)  11.1 us
  transfers between devices with their start and end apart: 5, of which 3 were waited for; matrix products, arithmetic and copies ran while one was open for 8% of the time, Pallas kernels for 0%

commit v1 on v0

--- a/solution.py
+++ b/solution.py
@@ -6,6 +6,18 @@
 REPLICA_COUNT = 64
 NS_ITERS = 5
 DIFFUSION = (0.05, 0.15)
+
+
+def gather_by_bits(x, axis, dim):
+    ways, here = (lax.axis_size(axis), lax.axis_index(axis))
+    grown, reach = (x, 1)
+    while reach < ways:
+        theirs = lax.ppermute(grown, axis, [(d, d ^ reach) for d in range(ways)])
+        mine_first = jnp.concatenate([grown, theirs], axis=dim)
+        theirs_first = jnp.concatenate([theirs, grown], axis=dim)
+        grown = jnp.where(here & reach == 0, mine_first, theirs_first)
+        reach = 2 * reach
+    return grown
 
 
 def padded(value, sides, width):
@@ -112,7 +124,7 @@
     local_obs = jnp.take(raveled_vector, obs_index, axis=1)
     slot_number = jnp.arange(capacity, dtype=jnp.int32)
     slot_weight = obs_weight * (slot_number < obs_count[0]).astype(jnp.float32)
-    gathered = lax.all_gather(local_obs, "mem", axis=0, tiled=True)
+    gathered = gather_by_bits(local_obs, "mem", 0)
     gram, drive = shard_terms(gathered, slot_weight, obs_value)
     gram, drive = lax.psum((gram, drive), "space")
     transform = ensemble_weights(gram, drive)

time: 221 us -> 195 us (0.88)
  waiting for transfers between devices: 31.5 us -> 16.1 us
  local copies, waits for them, and re-layouts: 91.4 us -> 84.6 us
  blocking collectives: 55.3 us -> 49.3 us
    all_to_all x1, waiting for transfers between devices: 21.9 us -> 0.01 us  [local(): lax.all_to_all(state, 'mem', split_axis=3, concat_axis=0, tiled=True)]
    unnamed x35 -> x27, local copies, waits for them, and re-layouts: 39.1 us -> 30.2 us
    all_gather x1 -> x0, blocking collectives: 7.17 us -> none  [local(): gathered = lax.all_gather(local_obs, 'mem', axis=0, tiled=True)]
    ppermute x2, waiting for transfers between devices: 1.18 us -> 4.06 us  [padded(): before = lax.ppermute(last, axis, up)]
    ppermute x2, waiting for transfers between devices: 8.44 us -> 10.7 us  [padded(): after = lax.ppermute(initial, axis, down)]
  transfers between devices with their start and end apart: 5 -> 7, of which waited for: 3 -> 5; matrix products, arithmetic and copies ran while one was open for 8% -> 18% of each run, Pallas kernels for 0% -> 0%
where the time goes in v1:
time: 195 us; the launch traced here: 194 us
  local copies, waits for them, and re-layouts  84.6 us (43%)
  blocking collectives  49.3 us (25%)
  other arithmetic  18.4 us (9%)
  starting transfers between devices  17.7 us (9%)
  waiting for transfers between devices  16.1 us (8%)
  matrix products  5.85 us (3%)
    unnamed x27, local copies, waits for them, and re-layouts  30.2 us
    all_to_all x1, blocking collectives, local(): lax.all_to_all(analysed, 'mem', split_axis=0, concat_axis=3, tiled=True)  28.7 us
    psum x1, blocking collectives, local(): gram, drive = lax.psum((gram, drive), 'space')  20.5 us
    add x2, local copies, waits for them, and re-layouts, advance(): center - wind_rows[0] * grad_row - wind_rows[1] * grad_col  19.5 us
    gather x1, local copies, waits for them, and re-layouts, local(): local_obs = jnp.take(raveled_vector, obs_index, axis=1)  13.4 us
    all_to_all x3, local copies, waits for them, and re-layouts, local(): lax.all_to_all(state, 'mem', split_axis=3, concat_axis=0, tiled=True)  12.3 us
    ppermute x2, waiting for transfers between devices, padded(): after = lax.ppermute(initial, axis, down)  10.7 us
    ppermute x2, starting transfers between devices, padded(): before = lax.ppermute(last, axis, up)  9.72 us
  transfers between devices with their start and end apart: 7, of which 5 were waited for; matrix products, arithmetic and copies ran while one was open for 18% of the time, Pallas kernels for 0%

profile of v1, /device:TPU:0, one launch (start us, length us, event | category | flops | bytes accessed | tf_op | source)
XLA Modules:
  0.0 194.2 jit_solution(15582293035407389983)
XLA Ops:
  0.0 2.8 %fusion.47 = (f32[16,2,2,2048]{3,2,1,0:T(2,128)S(1)}, f32[16,2,2,2048]{3,2,1,0:T(2,128)S(1)}) fusion(f32[16,2,8,2048]{3,2,1,0:T(8,128)} %param.10), kind=kLoop, calls=%fused_computation.82 | loop fusion | bytes 2097152 | tf_op jit(solution)/shard_map/slice | solution.py:29
  2.9 0.3 copy.70
  3.2 5.0 %collective-permute-start.1 = (f32[16,2,2,2048]{3,0,2,1:T(8,128)S(1)}, f32[16,2,2,2048]{3,0,2,1:T(8,128)S(1)}, u32[]{:S(2)}, u32[]{:S(2)}) collective-permute-start(f32[16,2,2,2048]{3,0,2,1:T(8,128)S(1)} %copy.70), channel_id=1, source_target_pairs={{0,4},{4,8},{8,12},{1,5},{5,9},{9,13},{2,6},{6,10},{10,14},{3,7},{... | collective-permute-start | bytes 1572872 | tf_op jit(solution)/shard_map/ppermute | solution.py:30
  8.1 0.3 copy.71
  8.5 1.3 collective-permute-start
  9.8 0.8 fusion.46
  10.6 0.8 fusion.45
  11.4 1.2 copy.72
  12.7 1.2 copy.73
  13.9 1.2 copy.74
  15.1 1.2 copy.75
  16.4 2.9 %collective-permute-done.1 = f32[16,2,2,2048]{3,0,2,1:T(8,128)S(1)} collective-permute-done((f32[16,2,2,2048]{3,0,2,1:T(8,128)S(1)}, f32[16,2,2,2048]{3,0,2,1:T(8,128)S(1)}, u32[]{:S(2)}, u32[]{:S(2)}) %collective-permute-start.1) | collective-permute-done | bytes 524320 | tf_op jit(solution)/shard_map/ppermute | solution.py:30
  19.3 1.2 constant_dynamic-update-slice_fusion.1
  20.5 3.2 %collective-permute-done = f32[16,2,2,2048]{3,0,2,1:T(8,128)S(1)} collective-permute-done((f32[16,2,2,2048]{3,0,2,1:T(8,128)S(1)}, f32[16,2,2,2048]{3,0,2,1:T(8,128)S(1)}, u32[]{:S(2)}, u32[]{:S(2)}) %collective-permute-start) | collective-permute-done | bytes 524320 | tf_op jit(solution)/shard_map/ppermute | solution.py:31
  23.8 4.0 %fusion.15 = f32[16,2,8,2048]{3,0,2,1:T(8,128)S(1)} fusion(f32[16,2,10,2048]{3,0,2,1:T(8,128)S(1)} %get-tuple-element.69, f32[16,2,10,2048]{3,0,2,1:T(8,128)S(1)} %constant_dynamic-update-slice_fusion, f32[16,2,8,2046]{3,0,2,1:T(8,128)S(1)} %copy.72, f32[16,2,8,2046]{3,0,2,1:T(8,128)S(1)} %copy.73, f32[16,2,8,2047]{3,0,2,1:T(8,128)S(1)} %copy.74, ...), kind=kLoop, calls=%fused_computation.25 | loop fusion | flops 9961472 | bytes 21096456 | tf_op jit(solution)/shard_map/add | solution.py:58
  27.7 0.8 fusion.42
  28.6 1.3 collective-permute-start.2
  29.9 4.8 %collective-permute-start.3 = (f32[16,2,2,2048]{3,0,2,1:T(8,128)S(1)}, f32[16,2,2,2048]{3,0,2,1:T(8,128)S(1)}, u32[]{:S(2)}, u32[]{:S(2)}) collective-permute-start(f32[16,2,2,2048]{3,0,2,1:T(8,128)S(1)} %get-tuple-element.61), channel_id=1, source_target_pairs={{0,4},{4,8},{8,12},{1,5},{5,9},{9,13},{2,6},{6,10},{10,14},{3,7},{... | collective-permute-start | bytes 1572872 | tf_op jit(solution)/shard_map/ppermute | solution.py:30
  34.7 0.8 fusion.43
  35.4 7.5 %collective-permute-done.2 = f32[16,2,2,2048]{3,0,2,1:T(8,128)S(1)} collective-permute-done((f32[16,2,2,2048]{3,0,2,1:T(8,128)S(1)}, f32[16,2,2,2048]{3,0,2,1:T(8,128)S(1)}, u32[]{:S(2)}, u32[]{:S(2)}) %collective-permute-start.2) | collective-permute-done | bytes 524320 | tf_op jit(solution)/shard_map/ppermute | solution.py:31
  43.0 1.2 collective-permute-done.3
  44.1 2.5 %fusion.10 = f32[16,2,8,2048]{3,0,2,1:T(8,128)S(1)} fusion(f32[16,2,8,2048]{3,0,2,1:T(8,128)S(1)} %fusion.15, f32[16,2,2,2048]{3,0,2,1:T(8,128)S(1)} %collective-permute-done.3, f32[16,2,2,2048]{3,0,2,1:T(8,128)S(1)} %collective-permute-done.2, f32[16,2,8,2046]{3,0,2,1:T(8,128)S(1)} %get-tuple-element.59, f32[16,2,8,2046]{3,0,2,1:T(8,128)S(1)} %get-tuple-element.58, ...), kind=kLoop, calls=%fused_computation.18 | loop fusion | flops 12058624 | bytes 13756424 | tf_op jit(solution)/shard_map/add | solution.py:58
  46.7 8.5 %copy.50 = f32[16,2,8,2048]{0,3,2,1:T(8,128)} copy(f32[16,2,8,2048]{3,0,2,1:T(8,128)S(1)} %fusion.10) | data formatting | bytes 4194304 | tf_op jit(solution)/shard_map/add | solution.py:58
  55.2 13.4 %gather_fusion = f32[2048,16]{1,0:T(8,128)} fusion(f32[16,32768]{0,1:T(8,128)} %bitcast.70, s32[2048]{0:T(1024)S(1)} %fusion.35), kind=kCustom, calls=%fused_computation | custom fusion | bytes 270336 | tf_op jit(solution)/shard_map/jit(_take)/gather | solution.py:124
  68.6 1.6 select_bitcast_fusion
  70.2 0.3 copy.52
  70.5 1.3 collective-permute-done.4
  71.9 1.6 collective-permute-start.5
  74.1 11.1 %copy.55 = f32[16,2,8,2048]{0,2,1,3:T(8,128)} copy(f32[16,2,8,2048]{3,0,2,1:T(8,128)S(1)} %fusion.10) | data formatting | bytes 4194304 | tf_op jit(solution)/shard_map/add | solution.py:58
  85.2 10.1 %reshape.58 = f32[4,1,131072]{2,1,0:T(1,128)} reshape(f32[2048,2,8,16]{3,2,1,0:T(8,128)} %bitcast.68) | data formatting | bytes 4194304
  95.3 3.7 %all-to-all-start = ((f32[4,1,131072]{2,1,0:T(1,128)}), f32[4,1,131072]{2,1,0:T(1,128)S(1)}, u32[]{:S(2)}, u32[]{:S(2)}) async-start(f32[4,1,131072]{2,1,0:T(1,128)} %reshape.58), calls=%async_computation | async-start | bytes 4194304 | tf_op jit(solution)/shard_map/all_to_all | solution.py:132
  99.1 0.6 fusion.18
  99.7 0.5 convolution_bitcast_fusion.2
  100.3 20.5 %all-reduce.8 = (f32[64,64]{1,0:T(8,128)S(1)}, f32[64]{0:T(128)S(1)}) all-reduce(f32[64,64]{1,0:T(8,128)S(1)} %fusion.18, f32[64]{0:T(128)S(1)} %convolution_bitcast_fusion.2), channel_id=1, replica_groups=mesh['parts'=2,'space'=4,'mem'=4] {'space'}, use_global_device_ids=true, to_apply=%region_1.2 | all-reduce | flops 4160 | bytes 33280 | tf_op jit(solution)/shard_map/psum | solution.py:129
  120.8 0.6 multiply_reduce_fusion
  122.2 3.4 %while.13 = (s32[]{:T(128)}, f32[64,64]{0,1:T(8,128)S(1)}, f32[64,64]{1,0:T(8,128)S(1)}, s32[]{:T(128)}) while((s32[]{:T(128)}, f32[64,64]{0,1:T(8,128)S(1)}, f32[64,64]{1,0:T(8,128)S(1)}, s32[]{:T(128)}) %tuple.37), condition=%wide.region_4.5_spmd.clone, body=%wide.region_3.4_spmd.clone.sunk | while | flops 9453570 | bytes 213045 | solution.py:104
  122.2 0.2 fusion.71
  122.4 0.2 fusion.72
  122.6 0.2 convolution_bitcast_fusion.4
  122.9 0.2 fusion.71
  123.1 0.2 fusion.72
  123.3 0.2 convolution_bitcast_fusion.4
  123.5 0.2 fusion.71
  123.7 0.2 fusion.72
  123.9 0.2 convolution_bitcast_fusion.4
  124.2 0.2 fusion.71
  124.4 0.2 fusion.72
  124.5 0.2 convolution_bitcast_fusion.4
  124.8 0.2 fusion.71
  125.0 0.2 fusion.72
  125.2 0.2 convolution_bitcast_fusion.4
  125.7 0.2 fusion.33
  126.1 1.3 copy-done.1
  127.4 0.5 broadcast.101
  127.9 7.7 %reduce.1 = f32[4,131072]{1,0:T(4,128)S(1)} reduce(f32[4,1,131072]{2,1,0:T(1,128)} %copy-done.1, f32[]{:T(128)} %broadcast.101), dimensions={1}, to_apply=%all_to_all.26.reduce_sub_computation | reduce | bytes 4194308 | tf_op jit(solution)/shard_map/all_to_all | solution.py:132
  135.6 11.5 %reshape.59 = f32[2048,2,8,16]{3,2,1,0:T(8,128)} reshape(f32[4,131072]{1,0:T(4,128)S(1)} %reduce.1) | data formatting | bytes 4194304
  147.2 10.2 %copy.56 = f32[16,2,8,4,512]{4,2,1,0,3:T(8,128)S(1)} copy(f32[16,2,8,4,512]{0,2,1,4,3:T(8,128)} %bitcast.69) | data formatting | bytes 4194304 | tf_op jit(solution)/shard_map/all_to_all | solution.py:132
  157.6 1.5 all_to_all.29
  159.1 1.7 subtract_convert_fusion
  160.8 0.4 copy.64
  161.2 1.5 convolution_add_fusion
  162.7 1.2 copy.59
  163.9 28.7 %all_to_all.36 = f32[64,2,8,512]{3,2,1,0:T(8,128)S(1)} all-to-all(f32[64,2,8,512]{3,2,1,0:T(8,128)S(1)} %copy.59), channel_id=1, replica_groups=mesh['parts'=2,'space'=4,'mem'=4] {'mem'}, dimensions={0} | all-to-all | bytes 4194304 | tf_op jit(solution)/shard_map/all_to_all | solution.py:141
  192.6 1.5 copy.60
  (43 shorter events, 0.8 us)
Async XLA Ops:
  0.0 9.8 %copy-start = (f32[16,2,8,2048]{3,2,1,0:T(8,128)S(1)}, f32[16,2,8,2048]{3,2,1,0:T(8,128)}, u32[]{:S(2)}) copy-start(f32[16,2,8,2048]{3,2,1,0:T(8,128)} %param.10) | copy-start | bytes 6291460
  3.2 16.1 %collective-permute-start.1 = (f32[16,2,2,2048]{3,0,2,1:T(8,128)S(1)}, f32[16,2,2,2048]{3,0,2,1:T(8,128)S(1)}, u32[]{:S(2)}, u32[]{:S(2)}) collective-permute-start(f32[16,2,2,2048]{3,0,2,1:T(8,128)S(1)} %copy.70), channel_id=1, source_target_pairs={{0,4},{4,8},{8,12},{1,5},{5,9},{9,13},{2,6},{6,10},{10,14},{3,7},{... | collective-permute-start | bytes 1572872 | tf_op jit(solution)/shard_map/ppermute | solution.py:30
  8.5 15.3 %collective-permute-start = (f32[16,2,2,2048]{3,0,2,1:T(8,128)S(1)}, f32[16,2,2,2048]{3,0,2,1:T(8,128)S(1)}, u32[]{:S(2)}, u32[]{:S(2)}) collective-permute-start(f32[16,2,2,2048]{3,0,2,1:T(8,128)S(1)} %copy.71), channel_id=1, source_target_pairs={{4,0},{8,4},{12,8},{5,1},{9,5},{13,9},{6,2},{10,6},{14,10},{7,3},{... | collective-permute-start | bytes 1572872 | tf_op jit(solution)/shard_map/ppermute | solution.py:31
  10.6 0.8 copy-start.3
  15.1 1.2 copy-start.2
  19.3 4.5 %copy-start.6 = (f32[2]{0:T(128)S(1)}, f32[2]{0:T(128)}, u32[]{:S(2)}) copy-start(f32[2]{0:T(128)} %constant.60.clone) | copy-start | bytes 28
  28.6 14.4 %collective-permute-start.2 = (f32[16,2,2,2048]{3,0,2,1:T(8,128)S(1)}, f32[16,2,2,2048]{3,0,2,1:T(8,128)S(1)}, u32[]{:S(2)}, u32[]{:S(2)}) collective-permute-start(f32[16,2,2,2048]{3,0,2,1:T(8,128)S(1)} %get-tuple-element.60), channel_id=1, source_target_pairs={{4,0},{8,4},{12,8},{5,1},{9,5},{13,9},{6,2},{10,6},{14,10},{7,3},{... | collective-permute-start | bytes 1572872 | tf_op jit(solution)/shard_map/ppermute | solution.py:31
  29.9 14.2 %collective-permute-start.3 = (f32[16,2,2,2048]{3,0,2,1:T(8,128)S(1)}, f32[16,2,2,2048]{3,0,2,1:T(8,128)S(1)}, u32[]{:S(2)}, u32[]{:S(2)}) collective-permute-start(f32[16,2,2,2048]{3,0,2,1:T(8,128)S(1)} %get-tuple-element.61), channel_id=1, source_target_pairs={{0,4},{4,8},{8,12},{1,5},{5,9},{9,13},{2,6},{6,10},{10,14},{3,7},{... | collective-permute-start | bytes 1572872 | tf_op jit(solution)/shard_map/ppermute | solution.py:30
  68.6 5.5 %copy-start.4 = (f32[2048]{0:T(1024)S(1)}, f32[2048]{0:T(1024)}, u32[]{:S(2)}) copy-start(f32[2048]{0:T(1024)} %param.15) | copy-start | bytes 24580
  70.5 1.4 collective-permute-start.4
  71.9 27.2 %collective-permute-start.5 = (f32[32,2048]{1,0:T(8,128)S(1)}, f32[32,2048]{1,0:T(8,128)S(1)}, u32[]{:S(2)}, u32[]{:S(2)}) collective-permute-start(f32[32,2048]{1,0:T(8,128)S(1)} %maximum_select_fusion.1), channel_id=1, source_target_pairs={{0,2},{1,3},{2,0},{3,1},{4,6},{5,7},{6,4},{7,5},{8,10},{9,11},{10,... | collective-permute-start | bytes 786440 | tf_op jit(solution)/shard_map/ppermute | solution.py:15
  95.3 3.8 %copy-start.5 = (f32[2048]{0:T(1024)S(1)}, f32[2048]{0:T(1024)}, u32[]{:S(2)}) copy-start(f32[2048]{0:T(1024)} %param.14) | copy-start | bytes 24580
  95.3 30.7 %all-to-all-start = ((f32[4,1,131072]{2,1,0:T(1,128)}), f32[4,1,131072]{2,1,0:T(1,128)S(1)}, u32[]{:S(2)}, u32[]{:S(2)}) async-start(f32[4,1,131072]{2,1,0:T(1,128)} %reshape.58), calls=%async_computation | async-start | bytes 4194304 | tf_op jit(solution)/shard_map/all_to_all | solution.py:132
  126.0 1.3 copy-start.1
